TPU v7x, 32 devices: a whole 2x2x4 slice. The times are simulated.
32 devices in a mesh: slab: 8 (over z, x), row: 4 (over y, core).
Axes of the slice: x: 2, y: 2, z: 4, core: 2. Of those that a mesh axis runs over, the one named last changes fastest.
Arguments:
- edge_weights: int32 [3, 16, 32, 512], P(None, 'slab', 'row'), may hold values from 1 to 15
- seeds: int32 [16, 32, 512], P('slab', 'row'), may hold values from -8 to 7
- supervoxel: int32 [16, 32, 512], P('slab', 'row'), may hold values from 0 to 127
- coarse_blocks: float32 [4, 1024, 1024], P('row', 'slab'), as said below
Outputs:
- potentials: float32 [8, 16, 32, 512], P(None, 'slab', 'row')
Inputs may be any that keep to these rules, and one draw needn't show every extreme that they name: `seeds`: a negative value marks an unseeded voxel. `coarse_blocks`: the entries named by dc lie between 0.6 and 1.2 times 2 * 8 * 4.
All inputs are finite; a program needn't handle non-finite values.
Results may differ from a plain program's by a relative error of at most 0.00024.
Values sent between devices are 32-bit elements; how exact they have to be, the bound alone decides.
No kernel may reach another device: no remote copies, remote signals or barrier semaphores. Data moves between devices by JAX's collectives and lax.ppermute only.
A program may use at most 64 MiB of HBM per device.

v0:
```python
import math
import jax
import jax.numpy as jnp
from jax import lax
from jax.sharding import PartitionSpec as P

LABELS = 8
CZ = 2
CY = 8
NX = 512
CC = 128
CYCLES = 2
prior_mass = 0.25
seed_weight = 4.0
smooth_step = 0.8
coarse_step = 0.7
weight_unit = 0.125


def padded(cells, sides, width):
    for axis, dim in sides:
        count = lax.axis_size(axis)
        ends = count - 1
        head = lax.slice_in_dim(cells, 0, width, axis=dim)
        tail = lax.slice_in_dim(cells, cells.shape[dim] - width, cells.shape[dim], axis=dim)
        cells = jnp.concatenate(
            [
                lax.ppermute(tail, axis, [(i, (i + 1) % count) for i in range(ends)]),
                cells,
                lax.ppermute(head, axis, [((i + 1) % count, i) for i in range(ends)]),
            ],
            axis=dim,
        )
    return cells


def shifted(block, axis, distance):
    devices = range(lax.axis_size(axis))
    route = [(i - distance, i) for i in devices if i - distance in devices]
    return lax.ppermute(block, axis, route)


def lower_x(a):
    return jnp.pad(a[..., :-1], [(0, 0)] * (a.ndim - 1) + [(1, 0)])


def upper_x(a):
    return jnp.pad(a[..., 1:], [(0, 0)] * (a.ndim - 1) + [(0, 1)])


def crop(a, margin):
    return a[..., margin : a.shape[-3] - margin, margin : a.shape[-2] - margin, :]


def rim_one(field):
    return padded(field, (("slab", 1), ("row", 2)), 1)


def per_device(edge_weights, seeds, supervoxel, coarse_blocks):
    n_slab = lax.axis_size("slab")
    n_row = lax.axis_size("row")
    group = min(16, n_slab)
    sections = n_slab // group
    slab_pos = lax.axis_index("slab")
    row_pos = lax.axis_index("row")
    stacked = jnp.concatenate([edge_weights, seeds[None]], axis=0)
    lower_plane = shifted(edge_weights[0, -1:], "slab", 1)
    lower_row = shifted(edge_weights[1, :, -1:], "row", 1)
    framed = jnp.pad(stacked, ((0, 0), (1, 1), (1, 1), (0, 0)))
    framed = framed.at[0, :1, 1:-1].set(lower_plane)
    framed = framed.at[1, 1:-1, :1].set(lower_row)
    width = (framed.shape[1] - CZ) // 2
    weights = framed[:3].astype(jnp.float32) * weight_unit
    plane_ids = slab_pos * CZ - width + jnp.arange(CZ + 2 * width, dtype=jnp.int32)
    line_ids = row_pos * CY - width + jnp.arange(CY + 2 * width, dtype=jnp.int32)
    keep_z = (plane_ids != CZ * n_slab - 1).astype(jnp.float32)[:, None, None]
    keep_y = (line_ids != CY * n_row - 1).astype(jnp.float32)[None, :, None]
    keep_x = (jnp.arange(NX) < NX - 1).astype(jnp.float32)[None, None, :]
    w_z = weights[0] * keep_z
    w_y = weights[1] * keep_y
    w_x = weights[2] * keep_x
    seed_inner = crop(framed[3], 1)
    inner_x = crop(w_x, 1)
    diag = (
        prior_mass
        + seed_weight * (seed_inner >= 0).astype(jnp.float32)
        + crop(w_z, 1)
        + crop(w_y, 1)
        + inner_x
        + w_z[:-2, 1:-1]
        + w_y[1:-1, :-2]
        + lower_x(inner_x)
    )
    label_ids = jnp.arange(LABELS, dtype=jnp.int32)
    source = seed_weight * (seed_inner[None] == label_ids[:, None, None, None]).astype(jnp.float32)

    def residual_on(frame, rim):
        margin = width - rim - 1
        face_z = crop(w_z, margin)
        face_y = crop(w_y, margin)
        face_x = crop(w_x, margin)[1:-1, 1:-1]
        centre = frame[:, 1:-1, 1:-1]
        near = face_z[1:-1, 1:-1] * frame[:, 2:, 1:-1] + face_z[:-2, 1:-1] * frame[:, :-2, 1:-1]
        near = (
            near + face_y[1:-1, 1:-1] * frame[:, 1:-1, 2:] + face_y[1:-1, :-2] * frame[:, 1:-1, :-2]
        )
        near = near + face_x * upper_x(centre) + lower_x(face_x) * lower_x(centre)
        local_diag = crop(diag, width - 1 - rim)
        local_source = crop(source, width - 1 - rim)
        return (local_source - (local_diag * centre - near), local_diag, centre)

    def sweep(field):
        change, local_diag, centre = residual_on(rim_one(field), 0)
        return centre + smooth_step * change / local_diag

    block_row = coarse_blocks[0]
    turn = slab_pos // sections
    section_id = slab_pos % sections
    own_block = lax.dynamic_slice_in_dim(block_row, turn * CC, CC, 1)
    coarse_diag = jnp.diagonal(own_block)
    cells = CZ * CY * NX
    span = math.gcd(cells, 2048)
    flat_ids = supervoxel.reshape(cells)
    coarse_ids = jnp.arange(CC, dtype=jnp.int32)
    field = jnp.zeros((LABELS, CZ, CY, NX), jnp.float32)
    for cycle in range(CYCLES):
        field = sweep(sweep(field))
        residual, unused_diag, unused_centre = residual_on(rim_one(field), 0)
        flat_rows = residual.reshape(LABELS, cells)

        def collect_block(index, total):
            piece = lax.dynamic_slice_in_dim(flat_rows, index * span, span, 1)
            piece_ids = lax.dynamic_slice_in_dim(flat_ids, index * span, span, 0)
            onehot = (piece_ids[:, None] == coarse_ids[None, :]).astype(jnp.float32)
            return total + jnp.dot(
                piece, onehot, precision=lax.Precision.HIGHEST, preferred_element_type=jnp.float32
            )

        coarse_rhs = lax.fori_loop(
            0, cells // span, collect_block, jnp.zeros((LABELS, CC), jnp.float32)
        )
        first = coarse_step * coarse_rhs / coarse_diag
        gathered = lax.all_gather(first, "slab", axis=1, tiled=True)
        arranged = gathered.reshape(LABELS, group, sections, CC)
        section = lax.dynamic_slice_in_dim(arranged, section_id, 1, 2).reshape(LABELS, group * CC)
        second = (
            first
            + coarse_step
            * (
                coarse_rhs
                - lax.dot_general(
                    section,
                    block_row,
                    (((1,), (1,)), ((), ())),
                    precision=lax.Precision.HIGHEST,
                    preferred_element_type=jnp.float32,
                )
            )
            / coarse_diag
        )
        correction = jnp.take(second, flat_ids, axis=1).reshape(LABELS, CZ, CY, NX)
        field = sweep(field + correction)
    return field


def solution(mesh):
    in_specs = (
        P(None, "slab", "row", None),
        P("slab", "row", None),
        P("slab", "row", None),
        P("row", "slab", None),
    )
    out_specs = P(None, "slab", "row", None)
    return jax.shard_map(
        per_device, mesh=mesh, in_specs=in_specs, out_specs=out_specs, check_vma=False
    )
```

profile of v0, /device:TPU:6, one launch (start us, length us, event | category | flops | bytes accessed | tf_op | source)
XLA Modules:
  0.0 296.9 jit_solution(196694166765577341)
XLA Ops:
  0.0 2.6 collective-permute-start.2
  2.6 4.3 %collective-permute-start.3 = (f32[8,1,8,512]{3,2,1,0:T(8,128)S(1)}, f32[8,1,8,512]{3,2,1,0:T(8,128)S(1)}, u32[]{:S(2)}, u32[]{:S(2)}) collective-permute-start(f32[8,1,8,512]{3,2,1,0:T(8,128)S(1)} %broadcast.145), channel_id=1, source_target_pairs={{0,4},{4,8},{8,12},{12,16},{16,20},{20,24},{24,28},{1,5},{5,9},{9,... | collective-permute-start | bytes 393224 | tf_op jit(solution)/shard_map/ppermute | solution.py:28
  7.6 2.5 collective-permute-start
  16.7 3.6 %collective-permute-start.4 = (f32[8,4,1,512]{3,2,1,0:T(1,128)S(1)}, f32[8,4,1,512]{3,2,1,0:T(1,128)S(1)}, u32[]{:S(2)}, u32[]{:S(2)}) collective-permute-start(f32[8,4,1,512]{3,2,1,0:T(1,128)S(1)} %get-tuple-element.286), channel_id=1, source_target_pairs={{1,0},{2,1},{3,2},{5,4},{6,5},{7,6},{9,8},{10,9},{11,10},{13,12},{... | collective-permute-start | bytes 196616 | tf_op jit(solution)/shard_map/ppermute | solution.py:30
  20.3 1.9 collective-permute-start.5
  22.4 3.6 %collective-permute-done.5 = f32[8,4,1,512]{3,2,1,0:T(1,128)S(1)} collective-permute-done((f32[8,4,1,512]{3,2,1,0:T(1,128)S(1)}, f32[8,4,1,512]{3,2,1,0:T(1,128)S(1)}, u32[]{:S(2)}, u32[]{:S(2)}) %collective-permute-start.5) | collective-permute-done | bytes 65568 | tf_op jit(solution)/shard_map/ppermute | solution.py:28
  26.2 3.3 %collective-permute-start.6 = (f32[8,1,8,512]{3,2,1,0:T(8,128)S(1)}, f32[8,1,8,512]{3,2,1,0:T(8,128)S(1)}, u32[]{:S(2)}, u32[]{:S(2)}) collective-permute-start(f32[8,1,8,512]{3,2,1,0:T(8,128)S(1)} %get-tuple-element.318), channel_id=1, source_target_pairs={{4,0},{8,4},{12,8},{16,12},{20,16},{24,20},{28,24},{5,1},{9,5},{13... | collective-permute-start | bytes 393224 | tf_op jit(solution)/shard_map/ppermute | solution.py:30
  29.5 3.5 %collective-permute-start.7 = (f32[8,1,8,512]{3,2,1,0:T(8,128)S(1)}, f32[8,1,8,512]{3,2,1,0:T(8,128)S(1)}, u32[]{:S(2)}, u32[]{:S(2)}) collective-permute-start(f32[8,1,8,512]{3,2,1,0:T(8,128)S(1)} %get-tuple-element.317), channel_id=1, source_target_pairs={{0,4},{4,8},{8,12},{12,16},{16,20},{20,24},{24,28},{1,5},{5,9},{9,... | collective-permute-start | bytes 393224 | tf_op jit(solution)/shard_map/ppermute | solution.py:28
  34.1 2.3 collective-permute-done.7
  36.5 1.9 collective-permute-start.8
  38.4 2.4 collective-permute-start.9
  41.0 3.0 %collective-permute-done.9 = f32[8,4,1,512]{3,2,1,0:T(1,128)S(1)} collective-permute-done((f32[8,4,1,512]{3,2,1,0:T(1,128)S(1)}, f32[8,4,1,512]{3,2,1,0:T(1,128)S(1)}, u32[]{:S(2)}, u32[]{:S(2)}) %collective-permute-start.9) | collective-permute-done | bytes 65568 | tf_op jit(solution)/shard_map/ppermute | solution.py:28
  44.3 1.9 collective-permute-start.10
  46.2 4.8 %collective-permute-start.11 = (f32[8,1,8,512]{3,2,1,0:T(8,128)S(1)}, f32[8,1,8,512]{3,2,1,0:T(8,128)S(1)}, u32[]{:S(2)}, u32[]{:S(2)}) collective-permute-start(f32[8,1,8,512]{3,2,1,0:T(8,128)S(1)} %get-tuple-element.313), channel_id=1, source_target_pairs={{0,4},{4,8},{8,12},{12,16},{16,20},{20,24},{24,28},{1,5},{5,9},{9,... | collective-permute-start | bytes 393224 | tf_op jit(solution)/shard_map/ppermute | solution.py:28
  55.6 2.4 collective-permute-start.13
  58.1 3.0 %collective-permute-done.13 = f32[8,4,1,512]{3,2,1,0:T(1,128)S(1)} collective-permute-done((f32[8,4,1,512]{3,2,1,0:T(1,128)S(1)}, f32[8,4,1,512]{3,2,1,0:T(1,128)S(1)}, u32[]{:S(2)}, u32[]{:S(2)}) %collective-permute-start.13) | collective-permute-done | bytes 65568 | tf_op jit(solution)/shard_map/ppermute | solution.py:28
  61.6 2.5 while.30
  64.1 31.9 %all_gather.6 = f32[8,1024]{1,0:T(8,128)S(1)} all-gather(f32[8,128]{1,0:T(8,128)S(1)} %multiply_divide_fusion.1), channel_id=1, replica_groups=mesh['slab'=8,'row'=4] {'slab'}, dimensions={1}, use_global_device_ids=true | all-gather | bytes 36864 | tf_op jit(solution)/shard_map/all_gather | solution.py:143
  96.6 27.9 %gather_fusion.1 = f32[8192,8]{1,0:T(8,128)} fusion(f32[8,128]{0,1:T(8,128)S(1)} %copy.9, s32[8192]{0:T(1024)S(1)} %fusion.122), kind=kCustom, calls=%fused_computation.clone | custom fusion | bytes 557056 | tf_op jit(solution)/shard_map/jit(_take)/gather | solution.py:161
  124.5 7.5 %broadcast_select_fusion.1 = f32[8192,8]{1,0:T(8,128)} fusion(f32[8192,8]{1,0:T(8,128)} %gather_fusion.1, pred[8192]{0:T(1024)(128)(4,1)S(1)} %compare_and_fusion), kind=kLoop, calls=%fused_computation.16 | loop fusion | flops 65536 | bytes 532480 | tf_op jit(solution)/shard_map/jit(_take)/select_n | solution.py:161
  131.9 2.8 copy.10
  134.8 3.3 %collective-permute-start.14 = (f32[8,1,8,512]{3,2,1,0:T(8,128)S(1)}, f32[8,1,8,512]{3,2,1,0:T(8,128)S(1)}, u32[]{:S(2)}, u32[]{:S(2)}) collective-permute-start(f32[8,1,8,512]{3,2,1,0:T(8,128)S(1)} %get-tuple-element.310), channel_id=1, source_target_pairs={{4,0},{8,4},{12,8},{16,12},{20,16},{24,20},{28,24},{5,1},{9,5},{13... | collective-permute-start | bytes 393224 | tf_op jit(solution)/shard_map/ppermute | solution.py:30
  138.1 3.5 %collective-permute-start.15 = (f32[8,1,8,512]{3,2,1,0:T(8,128)S(1)}, f32[8,1,8,512]{3,2,1,0:T(8,128)S(1)}, u32[]{:S(2)}, u32[]{:S(2)}) collective-permute-start(f32[8,1,8,512]{3,2,1,0:T(8,128)S(1)} %get-tuple-element.309), channel_id=1, source_target_pairs={{0,4},{4,8},{8,12},{12,16},{16,20},{20,24},{24,28},{1,5},{5,9},{9,... | collective-permute-start | bytes 393224 | tf_op jit(solution)/shard_map/ppermute | solution.py:28
  142.6 2.4 collective-permute-done.15
  147.0 2.4 collective-permute-start.17
  149.6 3.0 %collective-permute-done.17 = f32[8,4,1,512]{3,2,1,0:T(1,128)S(1)} collective-permute-done((f32[8,4,1,512]{3,2,1,0:T(1,128)S(1)}, f32[8,4,1,512]{3,2,1,0:T(1,128)S(1)}, u32[]{:S(2)}, u32[]{:S(2)}) %collective-permute-start.17) | collective-permute-done | bytes 65568 | tf_op jit(solution)/shard_map/ppermute | solution.py:28
  152.9 1.9 collective-permute-start.18
  154.8 4.8 %collective-permute-start.19 = (f32[8,1,8,512]{3,2,1,0:T(8,128)S(1)}, f32[8,1,8,512]{3,2,1,0:T(8,128)S(1)}, u32[]{:S(2)}, u32[]{:S(2)}) collective-permute-start(f32[8,1,8,512]{3,2,1,0:T(8,128)S(1)} %get-tuple-element.305), channel_id=1, source_target_pairs={{0,4},{4,8},{8,12},{12,16},{16,20},{20,24},{24,28},{1,5},{5,9},{9,... | collective-permute-start | bytes 393224 | tf_op jit(solution)/shard_map/ppermute | solution.py:28
  164.2 2.4 collective-permute-start.21
  166.7 3.0 %collective-permute-done.21 = f32[8,4,1,512]{3,2,1,0:T(1,128)S(1)} collective-permute-done((f32[8,4,1,512]{3,2,1,0:T(1,128)S(1)}, f32[8,4,1,512]{3,2,1,0:T(1,128)S(1)}, u32[]{:S(2)}, u32[]{:S(2)}) %collective-permute-start.21) | collective-permute-done | bytes 65568 | tf_op jit(solution)/shard_map/ppermute | solution.py:28
  172.0 5.3 %collective-permute-start.23 = (f32[8,1,8,512]{3,2,1,0:T(8,128)S(1)}, f32[8,1,8,512]{3,2,1,0:T(8,128)S(1)}, u32[]{:S(2)}, u32[]{:S(2)}) collective-permute-start(f32[8,1,8,512]{3,2,1,0:T(8,128)S(1)} %get-tuple-element.301), channel_id=1, source_target_pairs={{0,4},{4,8},{8,12},{12,16},{16,20},{20,24},{24,28},{1,5},{5,9},{9,... | collective-permute-start | bytes 393224 | tf_op jit(solution)/shard_map/ppermute | solution.py:28
  179.9 1.9 collective-permute-start.24
  181.9 2.4 collective-permute-start.25
  184.4 3.0 %collective-permute-done.25 = f32[8,4,1,512]{3,2,1,0:T(1,128)S(1)} collective-permute-done((f32[8,4,1,512]{3,2,1,0:T(1,128)S(1)}, f32[8,4,1,512]{3,2,1,0:T(1,128)S(1)}, u32[]{:S(2)}, u32[]{:S(2)}) %collective-permute-start.25) | collective-permute-done | bytes 65568 | tf_op jit(solution)/shard_map/ppermute | solution.py:28
  189.7 5.2 %collective-permute-start.27 = (f32[8,1,8,512]{3,2,1,0:T(8,128)S(1)}, f32[8,1,8,512]{3,2,1,0:T(8,128)S(1)}, u32[]{:S(2)}, u32[]{:S(2)}) collective-permute-start(f32[8,1,8,512]{3,2,1,0:T(8,128)S(1)} %get-tuple-element.297), channel_id=1, source_target_pairs={{0,4},{4,8},{8,12},{12,16},{16,20},{20,24},{24,28},{1,5},{5,9},{9,... | collective-permute-start | bytes 393224 | tf_op jit(solution)/shard_map/ppermute | solution.py:28
  197.5 1.9 collective-permute-start.28
  199.5 2.4 collective-permute-start.29
  202.0 3.0 %collective-permute-done.29 = f32[8,4,1,512]{3,2,1,0:T(1,128)S(1)} collective-permute-done((f32[8,4,1,512]{3,2,1,0:T(1,128)S(1)}, f32[8,4,1,512]{3,2,1,0:T(1,128)S(1)}, u32[]{:S(2)}, u32[]{:S(2)}) %collective-permute-start.29) | collective-permute-done | bytes 65568 | tf_op jit(solution)/shard_map/ppermute | solution.py:28
  205.5 2.5 while.31
  208.0 30.0 %all_gather.7 = f32[8,1024]{1,0:T(8,128)S(1)} all-gather(f32[8,128]{1,0:T(8,128)S(1)} %multiply_divide_fusion), channel_id=1, replica_groups=mesh['slab'=8,'row'=4] {'slab'}, dimensions={1}, use_global_device_ids=true | all-gather | bytes 36864 | tf_op jit(solution)/shard_map/all_gather | solution.py:143
  238.6 27.9 %gather_fusion.2 = f32[8192,8]{1,0:T(8,128)} fusion(f32[8,128]{0,1:T(8,128)S(1)} %copy.11, s32[8192]{0:T(1024)S(1)} %fusion.122), kind=kCustom, calls=%fused_computation.1.clone | custom fusion | bytes 557056 | tf_op jit(solution)/shard_map/jit(_take)/gather | solution.py:161
  266.5 7.5 %broadcast_select_fusion = f32[8192,8]{1,0:T(8,128)} fusion(f32[8192,8]{1,0:T(8,128)} %gather_fusion.2, pred[8192]{0:T(1024)(128)(4,1)S(1)} %compare_and_fusion), kind=kLoop, calls=%fused_computation.15 | loop fusion | flops 65536 | bytes 532480 | tf_op jit(solution)/shard_map/jit(_take)/select_n | solution.py:161
  273.9 2.8 copy.12
  276.8 4.6 %collective-permute-start.30 = (f32[8,1,8,512]{3,2,1,0:T(8,128)S(1)}, f32[8,1,8,512]{3,2,1,0:T(8,128)S(1)}, u32[]{:S(2)}, u32[]{:S(2)}) collective-permute-start(f32[8,1,8,512]{3,2,1,0:T(8,128)S(1)} %get-tuple-element.294), channel_id=1, source_target_pairs={{4,0},{8,4},{12,8},{16,12},{20,16},{24,20},{28,24},{5,1},{9,5},{13... | collective-permute-start | bytes 393224 | tf_op jit(solution)/shard_map/ppermute | solution.py:30
  281.4 2.1 collective-permute-start.31
  284.6 3.7 %collective-permute-done.31 = f32[8,1,8,512]{3,2,1,0:T(8,128)S(1)} collective-permute-done((f32[8,1,8,512]{3,2,1,0:T(8,128)S(1)}, f32[8,1,8,512]{3,2,1,0:T(8,128)S(1)}, u32[]{:S(2)}, u32[]{:S(2)}) %collective-permute-start.31) | collective-permute-done | bytes 131104 | tf_op jit(solution)/shard_map/ppermute | solution.py:28
  290.3 2.4 collective-permute-start.33
  292.9 3.0 %collective-permute-done.33 = f32[8,4,1,512]{3,2,1,0:T(1,128)S(1)} collective-permute-done((f32[8,4,1,512]{3,2,1,0:T(1,128)S(1)}, f32[8,4,1,512]{3,2,1,0:T(1,128)S(1)}, u32[]{:S(2)}, u32[]{:S(2)}) %collective-permute-start.33) | collective-permute-done | bytes 65568 | tf_op jit(solution)/shard_map/ppermute | solution.py:28
  (115 shorter events, 42.8 us)
Async XLA Ops:
  0.0 13.8 %copy-start = (f32[1,128,1024]{2,1,0:T(8,128)S(1)}, f32[1,128,1024]{2,1,0:T(8,128)}, u32[]{:S(2)}) copy-start(f32[1,128,1024]{2,1,0:T(8,128)} %param.17) | copy-start | bytes 1572868
  0.0 16.5 %collective-permute-start.2 = (f32[8,1,8,512]{3,2,1,0:T(8,128)S(1)}, f32[8,1,8,512]{3,2,1,0:T(8,128)S(1)}, u32[]{:S(2)}, u32[]{:S(2)}) collective-permute-start(f32[8,1,8,512]{3,2,1,0:T(8,128)S(1)} %broadcast.145), channel_id=1, source_target_pairs={{4,0},{8,4},{12,8},{16,12},{20,16},{24,20},{28,24},{5,1},{9,5},{13... | collective-permute-start | bytes 393224 | tf_op jit(solution)/shard_map/ppermute | solution.py:30
  2.6 14.0 %collective-permute-start.3 = (f32[8,1,8,512]{3,2,1,0:T(8,128)S(1)}, f32[8,1,8,512]{3,2,1,0:T(8,128)S(1)}, u32[]{:S(2)}, u32[]{:S(2)}) collective-permute-start(f32[8,1,8,512]{3,2,1,0:T(8,128)S(1)} %broadcast.145), channel_id=1, source_target_pairs={{0,4},{4,8},{8,12},{12,16},{16,20},{20,24},{24,28},{1,5},{5,9},{9,... | collective-permute-start | bytes 393224 | tf_op jit(solution)/shard_map/ppermute | solution.py:28
  7.6 8.4 %collective-permute-start = (s32[1,8,512]{2,1,0:T(8,128)S(1)}, s32[1,8,512]{2,1,0:T(8,128)S(1)}, u32[]{:S(2)}, u32[]{:S(2)}) collective-permute-start(s32[1,8,512]{2,1,0:T(8,128)S(1)} %slice_bitcast_fusion.4), channel_id=1, source_target_pairs={{0,4},{4,8},{8,12},{12,16},{16,20},{20,24},{24,28},{1,5},{5,9},{9,... | collective-permute-start | bytes 49160 | tf_op jit(solution)/shard_map/ppermute | solution.py:40
  10.9 5.3 %collective-permute-start.1 = (s32[2,1,512]{2,1,0:T(1,128)S(1)}, s32[2,1,512]{2,1,0:T(1,128)S(1)}, u32[]{:S(2)}, u32[]{:S(2)}) collective-permute-start(s32[2,1,512]{2,1,0:T(1,128)S(1)} %slice_bitcast_fusion.5), channel_id=1, source_target_pairs={{0,1},{1,2},{2,3},{4,5},{5,6},{6,7},{8,9},{9,10},{10,11},{12,13},{... | collective-permute-start | bytes 12296 | tf_op jit(solution)/shard_map/ppermute | solution.py:40
  16.7 5.7 %collective-permute-start.4 = (f32[8,4,1,512]{3,2,1,0:T(1,128)S(1)}, f32[8,4,1,512]{3,2,1,0:T(1,128)S(1)}, u32[]{:S(2)}, u32[]{:S(2)}) collective-permute-start(f32[8,4,1,512]{3,2,1,0:T(1,128)S(1)} %get-tuple-element.286), channel_id=1, source_target_pairs={{1,0},{2,1},{3,2},{5,4},{6,5},{7,6},{9,8},{10,9},{11,10},{13,12},{... | collective-permute-start | bytes 196616 | tf_op jit(solution)/shard_map/ppermute | solution.py:30
  20.3 5.6 %collective-permute-start.5 = (f32[8,4,1,512]{3,2,1,0:T(1,128)S(1)}, f32[8,4,1,512]{3,2,1,0:T(1,128)S(1)}, u32[]{:S(2)}, u32[]{:S(2)}) collective-permute-start(f32[8,4,1,512]{3,2,1,0:T(1,128)S(1)} %get-tuple-element.287), channel_id=1, source_target_pairs={{0,1},{1,2},{2,3},{4,5},{5,6},{6,7},{8,9},{9,10},{10,11},{12,13},{... | collective-permute-start | bytes 196616 | tf_op jit(solution)/shard_map/ppermute | solution.py:28
  26.2 7.9 %collective-permute-start.6 = (f32[8,1,8,512]{3,2,1,0:T(8,128)S(1)}, f32[8,1,8,512]{3,2,1,0:T(8,128)S(1)}, u32[]{:S(2)}, u32[]{:S(2)}) collective-permute-start(f32[8,1,8,512]{3,2,1,0:T(8,128)S(1)} %get-tuple-element.318), channel_id=1, source_target_pairs={{4,0},{8,4},{12,8},{16,12},{20,16},{24,20},{28,24},{5,1},{9,5},{13... | collective-permute-start | bytes 393224 | tf_op jit(solution)/shard_map/ppermute | solution.py:30
  29.5 6.9 %collective-permute-start.7 = (f32[8,1,8,512]{3,2,1,0:T(8,128)S(1)}, f32[8,1,8,512]{3,2,1,0:T(8,128)S(1)}, u32[]{:S(2)}, u32[]{:S(2)}) collective-permute-start(f32[8,1,8,512]{3,2,1,0:T(8,128)S(1)} %get-tuple-element.317), channel_id=1, source_target_pairs={{0,4},{4,8},{8,12},{12,16},{16,20},{20,24},{24,28},{1,5},{5,9},{9,... | collective-permute-start | bytes 393224 | tf_op jit(solution)/shard_map/ppermute | solution.py:28
  36.5 4.5 %collective-permute-start.8 = (f32[8,4,1,512]{3,2,1,0:T(1,128)S(1)}, f32[8,4,1,512]{3,2,1,0:T(1,128)S(1)}, u32[]{:S(2)}, u32[]{:S(2)}) collective-permute-start(f32[8,4,1,512]{3,2,1,0:T(1,128)S(1)} %get-tuple-element.284), channel_id=1, source_target_pairs={{1,0},{2,1},{3,2},{5,4},{6,5},{7,6},{9,8},{10,9},{11,10},{13,12},{... | collective-permute-start | bytes 196616 | tf_op jit(solution)/shard_map/ppermute | solution.py:30
  38.4 5.6 %collective-permute-start.9 = (f32[8,4,1,512]{3,2,1,0:T(1,128)S(1)}, f32[8,4,1,512]{3,2,1,0:T(1,128)S(1)}, u32[]{:S(2)}, u32[]{:S(2)}) collective-permute-start(f32[8,4,1,512]{3,2,1,0:T(1,128)S(1)} %get-tuple-element.285), channel_id=1, source_target_pairs={{0,1},{1,2},{2,3},{4,5},{5,6},{6,7},{8,9},{9,10},{10,11},{12,13},{... | collective-permute-start | bytes 196616 | tf_op jit(solution)/shard_map/ppermute | solution.py:28
  44.3 7.8 %collective-permute-start.10 = (f32[8,1,8,512]{3,2,1,0:T(8,128)S(1)}, f32[8,1,8,512]{3,2,1,0:T(8,128)S(1)}, u32[]{:S(2)}, u32[]{:S(2)}) collective-permute-start(f32[8,1,8,512]{3,2,1,0:T(8,128)S(1)} %get-tuple-element.314), channel_id=1, source_target_pairs={{4,0},{8,4},{12,8},{16,12},{20,16},{24,20},{28,24},{5,1},{9,5},{13... | collective-permute-start | bytes 393224 | tf_op jit(solution)/shard_map/ppermute | solution.py:30
  46.2 7.3 %collective-permute-start.11 = (f32[8,1,8,512]{3,2,1,0:T(8,128)S(1)}, f32[8,1,8,512]{3,2,1,0:T(8,128)S(1)}, u32[]{:S(2)}, u32[]{:S(2)}) collective-permute-start(f32[8,1,8,512]{3,2,1,0:T(8,128)S(1)} %get-tuple-element.313), channel_id=1, source_target_pairs={{0,4},{4,8},{8,12},{12,16},{16,20},{20,24},{24,28},{1,5},{5,9},{9,... | collective-permute-start | bytes 393224 | tf_op jit(solution)/shard_map/ppermute | solution.py:28
  53.6 4.5 %collective-permute-start.12 = (f32[8,4,1,512]{3,2,1,0:T(1,128)S(1)}, f32[8,4,1,512]{3,2,1,0:T(1,128)S(1)}, u32[]{:S(2)}, u32[]{:S(2)}) collective-permute-start(f32[8,4,1,512]{3,2,1,0:T(1,128)S(1)} %get-tuple-element.282), channel_id=1, source_target_pairs={{1,0},{2,1},{3,2},{5,4},{6,5},{7,6},{9,8},{10,9},{11,10},{13,12},{... | collective-permute-start | bytes 196616 | tf_op jit(solution)/shard_map/ppermute | solution.py:30
  55.6 5.6 %collective-permute-start.13 = (f32[8,4,1,512]{3,2,1,0:T(1,128)S(1)}, f32[8,4,1,512]{3,2,1,0:T(1,128)S(1)}, u32[]{:S(2)}, u32[]{:S(2)}) collective-permute-start(f32[8,4,1,512]{3,2,1,0:T(1,128)S(1)} %get-tuple-element.283), channel_id=1, source_target_pairs={{0,1},{1,2},{2,3},{4,5},{5,6},{6,7},{8,9},{9,10},{10,11},{12,13},{... | collective-permute-start | bytes 196616 | tf_op jit(solution)/shard_map/ppermute | solution.py:28
  134.8 7.8 %collective-permute-start.14 = (f32[8,1,8,512]{3,2,1,0:T(8,128)S(1)}, f32[8,1,8,512]{3,2,1,0:T(8,128)S(1)}, u32[]{:S(2)}, u32[]{:S(2)}) collective-permute-start(f32[8,1,8,512]{3,2,1,0:T(8,128)S(1)} %get-tuple-element.310), channel_id=1, source_target_pairs={{4,0},{8,4},{12,8},{16,12},{20,16},{24,20},{28,24},{5,1},{9,5},{13... | collective-permute-start | bytes 393224 | tf_op jit(solution)/shard_map/ppermute | solution.py:30
  138.1 6.9 %collective-permute-start.15 = (f32[8,1,8,512]{3,2,1,0:T(8,128)S(1)}, f32[8,1,8,512]{3,2,1,0:T(8,128)S(1)}, u32[]{:S(2)}, u32[]{:S(2)}) collective-permute-start(f32[8,1,8,512]{3,2,1,0:T(8,128)S(1)} %get-tuple-element.309), channel_id=1, source_target_pairs={{0,4},{4,8},{8,12},{12,16},{16,20},{20,24},{24,28},{1,5},{5,9},{9,... | collective-permute-start | bytes 393224 | tf_op jit(solution)/shard_map/ppermute | solution.py:28
  145.1 4.5 %collective-permute-start.16 = (f32[8,4,1,512]{3,2,1,0:T(1,128)S(1)}, f32[8,4,1,512]{3,2,1,0:T(1,128)S(1)}, u32[]{:S(2)}, u32[]{:S(2)}) collective-permute-start(f32[8,4,1,512]{3,2,1,0:T(1,128)S(1)} %get-tuple-element.280), channel_id=1, source_target_pairs={{1,0},{2,1},{3,2},{5,4},{6,5},{7,6},{9,8},{10,9},{11,10},{13,12},{... | collective-permute-start | bytes 196616 | tf_op jit(solution)/shard_map/ppermute | solution.py:30
  147.0 5.6 %collective-permute-start.17 = (f32[8,4,1,512]{3,2,1,0:T(1,128)S(1)}, f32[8,4,1,512]{3,2,1,0:T(1,128)S(1)}, u32[]{:S(2)}, u32[]{:S(2)}) collective-permute-start(f32[8,4,1,512]{3,2,1,0:T(1,128)S(1)} %get-tuple-element.281), channel_id=1, source_target_pairs={{0,1},{1,2},{2,3},{4,5},{5,6},{6,7},{8,9},{9,10},{10,11},{12,13},{... | collective-permute-start | bytes 196616 | tf_op jit(solution)/shard_map/ppermute | solution.py:28
  152.9 7.8 %collective-permute-start.18 = (f32[8,1,8,512]{3,2,1,0:T(8,128)S(1)}, f32[8,1,8,512]{3,2,1,0:T(8,128)S(1)}, u32[]{:S(2)}, u32[]{:S(2)}) collective-permute-start(f32[8,1,8,512]{3,2,1,0:T(8,128)S(1)} %get-tuple-element.306), channel_id=1, source_target_pairs={{4,0},{8,4},{12,8},{16,12},{20,16},{24,20},{28,24},{5,1},{9,5},{13... | collective-permute-start | bytes 393224 | tf_op jit(solution)/shard_map/ppermute | solution.py:30
  154.8 7.3 %collective-permute-start.19 = (f32[8,1,8,512]{3,2,1,0:T(8,128)S(1)}, f32[8,1,8,512]{3,2,1,0:T(8,128)S(1)}, u32[]{:S(2)}, u32[]{:S(2)}) collective-permute-start(f32[8,1,8,512]{3,2,1,0:T(8,128)S(1)} %get-tuple-element.305), channel_id=1, source_target_pairs={{0,4},{4,8},{8,12},{12,16},{16,20},{20,24},{24,28},{1,5},{5,9},{9,... | collective-permute-start | bytes 393224 | tf_op jit(solution)/shard_map/ppermute | solution.py:28
  162.2 4.5 %collective-permute-start.20 = (f32[8,4,1,512]{3,2,1,0:T(1,128)S(1)}, f32[8,4,1,512]{3,2,1,0:T(1,128)S(1)}, u32[]{:S(2)}, u32[]{:S(2)}) collective-permute-start(f32[8,4,1,512]{3,2,1,0:T(1,128)S(1)} %get-tuple-element.278), channel_id=1, source_target_pairs={{1,0},{2,1},{3,2},{5,4},{6,5},{7,6},{9,8},{10,9},{11,10},{13,12},{... | collective-permute-start | bytes 196616 | tf_op jit(solution)/shard_map/ppermute | solution.py:30
  164.2 5.6 %collective-permute-start.21 = (f32[8,4,1,512]{3,2,1,0:T(1,128)S(1)}, f32[8,4,1,512]{3,2,1,0:T(1,128)S(1)}, u32[]{:S(2)}, u32[]{:S(2)}) collective-permute-start(f32[8,4,1,512]{3,2,1,0:T(1,128)S(1)} %get-tuple-element.279), channel_id=1, source_target_pairs={{0,1},{1,2},{2,3},{4,5},{5,6},{6,7},{8,9},{9,10},{10,11},{12,13},{... | collective-permute-start | bytes 196616 | tf_op jit(solution)/shard_map/ppermute | solution.py:28
  170.1 8.3 %collective-permute-start.22 = (f32[8,1,8,512]{3,2,1,0:T(8,128)S(1)}, f32[8,1,8,512]{3,2,1,0:T(8,128)S(1)}, u32[]{:S(2)}, u32[]{:S(2)}) collective-permute-start(f32[8,1,8,512]{3,2,1,0:T(8,128)S(1)} %get-tuple-element.302), channel_id=1, source_target_pairs={{4,0},{8,4},{12,8},{16,12},{20,16},{24,20},{28,24},{5,1},{9,5},{13... | collective-permute-start | bytes 393224 | tf_op jit(solution)/shard_map/ppermute | solution.py:30
  172.0 7.8 %collective-permute-start.23 = (f32[8,1,8,512]{3,2,1,0:T(8,128)S(1)}, f32[8,1,8,512]{3,2,1,0:T(8,128)S(1)}, u32[]{:S(2)}, u32[]{:S(2)}) collective-permute-start(f32[8,1,8,512]{3,2,1,0:T(8,128)S(1)} %get-tuple-element.301), channel_id=1, source_target_pairs={{0,4},{4,8},{8,12},{12,16},{16,20},{20,24},{24,28},{1,5},{5,9},{9,... | collective-permute-start | bytes 393224 | tf_op jit(solution)/shard_map/ppermute | solution.py:28
  179.9 4.5 %collective-permute-start.24 = (f32[8,4,1,512]{3,2,1,0:T(1,128)S(1)}, f32[8,4,1,512]{3,2,1,0:T(1,128)S(1)}, u32[]{:S(2)}, u32[]{:S(2)}) collective-permute-start(f32[8,4,1,512]{3,2,1,0:T(1,128)S(1)} %get-tuple-element.276), channel_id=1, source_target_pairs={{1,0},{2,1},{3,2},{5,4},{6,5},{7,6},{9,8},{10,9},{11,10},{13,12},{... | collective-permute-start | bytes 196616 | tf_op jit(solution)/shard_map/ppermute | solution.py:30
  181.9 5.6 %collective-permute-start.25 = (f32[8,4,1,512]{3,2,1,0:T(1,128)S(1)}, f32[8,4,1,512]{3,2,1,0:T(1,128)S(1)}, u32[]{:S(2)}, u32[]{:S(2)}) collective-permute-start(f32[8,4,1,512]{3,2,1,0:T(1,128)S(1)} %get-tuple-element.277), channel_id=1, source_target_pairs={{0,1},{1,2},{2,3},{4,5},{5,6},{6,7},{8,9},{9,10},{10,11},{12,13},{... | collective-permute-start | bytes 196616 | tf_op jit(solution)/shard_map/ppermute | solution.py:28
  187.8 8.2 %collective-permute-start.26 = (f32[8,1,8,512]{3,2,1,0:T(8,128)S(1)}, f32[8,1,8,512]{3,2,1,0:T(8,128)S(1)}, u32[]{:S(2)}, u32[]{:S(2)}) collective-permute-start(f32[8,1,8,512]{3,2,1,0:T(8,128)S(1)} %get-tuple-element.298), channel_id=1, source_target_pairs={{4,0},{8,4},{12,8},{16,12},{20,16},{24,20},{28,24},{5,1},{9,5},{13... | collective-permute-start | bytes 393224 | tf_op jit(solution)/shard_map/ppermute | solution.py:30
  189.7 7.8 %collective-permute-start.27 = (f32[8,1,8,512]{3,2,1,0:T(8,128)S(1)}, f32[8,1,8,512]{3,2,1,0:T(8,128)S(1)}, u32[]{:S(2)}, u32[]{:S(2)}) collective-permute-start(f32[8,1,8,512]{3,2,1,0:T(8,128)S(1)} %get-tuple-element.297), channel_id=1, source_target_pairs={{0,4},{4,8},{8,12},{12,16},{16,20},{20,24},{24,28},{1,5},{5,9},{9,... | collective-permute-start | bytes 393224 | tf_op jit(solution)/shard_map/ppermute | solution.py:28
  197.5 4.5 %collective-permute-start.28 = (f32[8,4,1,512]{3,2,1,0:T(1,128)S(1)}, f32[8,4,1,512]{3,2,1,0:T(1,128)S(1)}, u32[]{:S(2)}, u32[]{:S(2)}) collective-permute-start(f32[8,4,1,512]{3,2,1,0:T(1,128)S(1)} %get-tuple-element.274), channel_id=1, source_target_pairs={{1,0},{2,1},{3,2},{5,4},{6,5},{7,6},{9,8},{10,9},{11,10},{13,12},{... | collective-permute-start | bytes 196616 | tf_op jit(solution)/shard_map/ppermute | solution.py:30
  199.5 5.6 %collective-permute-start.29 = (f32[8,4,1,512]{3,2,1,0:T(1,128)S(1)}, f32[8,4,1,512]{3,2,1,0:T(1,128)S(1)}, u32[]{:S(2)}, u32[]{:S(2)}) collective-permute-start(f32[8,4,1,512]{3,2,1,0:T(1,128)S(1)} %get-tuple-element.275), channel_id=1, source_target_pairs={{0,1},{1,2},{2,3},{4,5},{5,6},{6,7},{8,9},{9,10},{10,11},{12,13},{... | collective-permute-start | bytes 196616 | tf_op jit(solution)/shard_map/ppermute | solution.py:28
  276.8 7.8 %collective-permute-start.30 = (f32[8,1,8,512]{3,2,1,0:T(8,128)S(1)}, f32[8,1,8,512]{3,2,1,0:T(8,128)S(1)}, u32[]{:S(2)}, u32[]{:S(2)}) collective-permute-start(f32[8,1,8,512]{3,2,1,0:T(8,128)S(1)} %get-tuple-element.294), channel_id=1, source_target_pairs={{4,0},{8,4},{12,8},{16,12},{20,16},{24,20},{28,24},{5,1},{9,5},{13... | collective-permute-start | bytes 393224 | tf_op jit(solution)/shard_map/ppermute | solution.py:30
  281.4 6.9 %collective-permute-start.31 = (f32[8,1,8,512]{3,2,1,0:T(8,128)S(1)}, f32[8,1,8,512]{3,2,1,0:T(8,128)S(1)}, u32[]{:S(2)}, u32[]{:S(2)}) collective-permute-start(f32[8,1,8,512]{3,2,1,0:T(8,128)S(1)} %get-tuple-element.293), channel_id=1, source_target_pairs={{0,4},{4,8},{8,12},{12,16},{16,20},{20,24},{24,28},{1,5},{5,9},{9,... | collective-permute-start | bytes 393224 | tf_op jit(solution)/shard_map/ppermute | solution.py:28
  288.4 4.5 %collective-permute-start.32 = (f32[8,4,1,512]{3,2,1,0:T(1,128)S(1)}, f32[8,4,1,512]{3,2,1,0:T(1,128)S(1)}, u32[]{:S(2)}, u32[]{:S(2)}) collective-permute-start(f32[8,4,1,512]{3,2,1,0:T(1,128)S(1)} %get-tuple-element.272), channel_id=1, source_target_pairs={{1,0},{2,1},{3,2},{5,4},{6,5},{7,6},{9,8},{10,9},{11,10},{13,12},{... | collective-permute-start | bytes 196616 | tf_op jit(solution)/shard_map/ppermute | solution.py:30
  290.3 5.6 %collective-permute-start.33 = (f32[8,4,1,512]{3,2,1,0:T(1,128)S(1)}, f32[8,4,1,512]{3,2,1,0:T(1,128)S(1)}, u32[]{:S(2)}, u32[]{:S(2)}) collective-permute-start(f32[8,4,1,512]{3,2,1,0:T(1,128)S(1)} %get-tuple-element.273), channel_id=1, source_target_pairs={{0,1},{1,2},{2,3},{4,5},{5,6},{6,7},{8,9},{9,10},{10,11},{12,13},{... | collective-permute-start | bytes 196616 | tf_op jit(solution)/shard_map/ppermute | solution.py:28
where the time goes:
time: 298 us; the launch traced here: 297 us
  starting transfers between devices  95.1 us (32%)
  local copies, waits for them, and re-layouts  66.9 us (22%)
  blocking collectives  61.9 us (21%)
  waiting for transfers between devices  46.4 us (16%)
  other arithmetic  19.8 us (7%)
  matrix products  5.65 us (2%)
    all_gather x2, blocking collectives, per_device(): gathered = lax.all_gather(first, 'slab', axis=1, tiled=True)  61.9 us
    gather x2, local copies, waits for them, and re-layouts, per_device(): correction = jnp.take(second, flat_ids, axis=1).reshape(LABELS, CZ, CY, NX)  55.7 us
    ppermute x16, starting transfers between devices, padded(): lax.ppermute(tail, axis, [(i, (i + 1) % count) for i in range(ends)])  52.2 us
    ppermute x16, waiting for transfers between devices, padded(): lax.ppermute(tail, axis, [(i, (i + 1) % count) for i in range(ends)])  39 us
    ppermute x16, starting transfers between devices, padded(): lax.ppermute(head, axis, [((i + 1) % count, i) for i in range(ends)])  38.5 us
    select_n x2, other arithmetic, per_device(): correction = jnp.take(second, flat_ids, axis=1).reshape(LABELS, CZ, CY, NX)  14.9 us
    ppermute x16, waiting for transfers between devices, padded(): lax.ppermute(head, axis, [((i + 1) % count, i) for i in range(ends)])  7.38 us
  transfers between devices with their start and end apart: 34, of which 22 were waited for; matrix products, arithmetic and copies ran while one was open for 2% of the time, Pallas kernels for 0%

commit v1 on v0

--- a/solution.py
+++ b/solution.py
@@ -15,6 +15,34 @@
 smooth_step = 0.8
 coarse_step = 0.7
 weight_unit = 0.125
+
+
+def tiles_produce(mine, in_dim):
+    mine = jnp.moveaxis(mine, 0, in_dim)
+    b_next = mine.shape
+    earlier = mine.reshape(
+        *b_next[:in_dim], b_next[in_dim] * b_next[in_dim + 1], *b_next[in_dim + 2 :]
+    )
+    return earlier
+
+
+def pair_joints(s0, mesh_name):
+    far_arr = s0[None]
+    degree = jax.lax.axis_size(mesh_name)
+    for ii in range(degree.bit_length() - 1):
+        answer = 1 << ii
+        main = jax.lax.ppermute(
+            far_arr, axis_name=mesh_name, perm=[(j, j ^ answer) for j in range(degree)]
+        )
+        finding = jnp.stack([far_arr, main])
+        aux = jax.lax.axis_index(mesh_name) >> ii & 1
+        far_arr = jnp.where(aux == 0, finding, finding[::-1]).reshape(-1, *s0.shape)
+    return far_arr
+
+
+def rest_samples_all(own_rows, local_values, dim_k):
+    passed = tiles_produce(pair_joints(own_rows, local_values), dim_k)
+    return passed
 
 
 def padded(cells, sides, width):
@@ -140,7 +168,7 @@
             0, cells // span, collect_block, jnp.zeros((LABELS, CC), jnp.float32)
         )
         first = coarse_step * coarse_rhs / coarse_diag
-        gathered = lax.all_gather(first, "slab", axis=1, tiled=True)
+        gathered = rest_samples_all(first, "slab", 1)
         arranged = gathered.reshape(LABELS, group, sections, CC)
         section = lax.dynamic_slice_in_dim(arranged, section_id, 1, 2).reshape(LABELS, group * CC)
         second = (

time: 298 us -> 260 us (0.87)
  blocking collectives: 61.9 us -> 0 us
  waiting for transfers between devices: 46.4 us -> 58.7 us
  starting transfers between devices: 95.1 us -> 106 us
    all_gather x2 -> x0, blocking collectives: 61.9 us -> none  [per_device(): gathered = lax.all_gather(first, 'slab', axis=1, tiled=True)]
    ppermute x0 -> x6, waiting for transfers between devices: none -> 13.8 us  [pair_joints(): jax.lax.ppermute(far_arr, axis_name=mesh_name, perm=[(j, j ^ answer) for...]
    ppermute x0 -> x6, starting transfers between devices: none -> 12.2 us  [pair_joints(): jax.lax.ppermute(far_arr, axis_name=mesh_name, perm=[(j, j ^ answer) for...]
    ppermute x16, starting transfers between devices: 38.5 us -> 35.5 us  [padded(): lax.ppermute(head, axis, [((i + 1) % count, i) for i in range(ends)])]
  transfers between devices with their start and end apart: 34 -> 40, of which waited for: 22 -> 28; matrix products, arithmetic and copies ran while one was open for 2% -> 2% of each run, Pallas kernels for 0% -> 0%
where the time goes in v1:
time: 260 us; the launch traced here: 257 us
  starting transfers between devices  106 us (41%)
  local copies, waits for them, and re-layouts  65.8 us (25%)
  waiting for transfers between devices  58.7 us (23%)
  other arithmetic  19.9 us (8%)
  matrix products  5.66 us (2%)
    gather x2, local copies, waits for them, and re-layouts, per_device(): correction = jnp.take(second, flat_ids, axis=1).reshape(LABELS, CZ, CY, NX)  55.4 us
    ppermute x16, starting transfers between devices, padded(): lax.ppermute(tail, axis, [(i, (i + 1) % count) for i in range(ends)])  54.1 us
    ppermute x16, waiting for transfers between devices, padded(): lax.ppermute(tail, axis, [(i, (i + 1) % count) for i in range(ends)])  36.7 us
    ppermute x16, starting transfers between devices, padded(): lax.ppermute(head, axis, [((i + 1) % count, i) for i in range(ends)])  35.5 us
    select_n x2, other arithmetic, per_device(): correction = jnp.take(second, flat_ids, axis=1).reshape(LABELS, CZ, CY, NX)  14.9 us
    ppermute x6, waiting for transfers between devices, pair_joints(): jax.lax.ppermute(far_arr, axis_name=mesh_name, perm=[(j, j ^ answer) for...  13.8 us
    ppermute x6, starting transfers between devices, pair_joints(): jax.lax.ppermute(far_arr, axis_name=mesh_name, perm=[(j, j ^ answer) for...  12.2 us
    ppermute x16, waiting for transfers between devices, padded(): lax.ppermute(head, axis, [((i + 1) % count, i) for i in range(ends)])  6.38 us
  transfers between devices with their start and end apart: 40, of which 28 were waited for; matrix products, arithmetic and copies ran while one was open for 2% of the time, Pallas kernels for 0%

profile of v1, /device:TPU:6, one launch (start us, length us, event | category | flops | bytes accessed | tf_op | source)
XLA Modules:
  0.0 257.4 jit_solution(11656950284326380178)
XLA Ops:
  0.0 2.6 %collective-permute-start.2 = (f32[8,1,8,512]{3,2,1,0:T(8,128)S(1)}, f32[8,1,8,512]{3,2,1,0:T(8,128)S(1)}, u32[]{:S(2)}, u32[]{:S(2)}) collective-permute-start(f32[8,1,8,512]{3,2,1,0:T(8,128)S(1)} %broadcast.145), channel_id=1, source_target_pairs={{4,0},{8,4},{12,8},{16,12},{20,16},{24,20},{28,24},{5,1},{9,5},{13... | collective-permute-start | bytes 393224 | tf_op jit(solution)/shard_map/ppermute | solution.py:58
  2.6 4.3 %collective-permute-start.3 = (f32[8,1,8,512]{3,2,1,0:T(8,128)S(1)}, f32[8,1,8,512]{3,2,1,0:T(8,128)S(1)}, u32[]{:S(2)}, u32[]{:S(2)}) collective-permute-start(f32[8,1,8,512]{3,2,1,0:T(8,128)S(1)} %broadcast.145), channel_id=1, source_target_pairs={{0,4},{4,8},{8,12},{12,16},{16,20},{20,24},{24,28},{1,5},{5,9},{9,... | collective-permute-start | bytes 393224 | tf_op jit(solution)/shard_map/ppermute | solution.py:56
  7.6 2.5 collective-permute-start
  16.3 1.9 collective-permute-start.4
  18.3 2.4 collective-permute-start.5
  20.8 3.1 %collective-permute-done.5 = f32[8,4,1,512]{3,2,1,0:T(1,128)S(1)} collective-permute-done((f32[8,4,1,512]{3,2,1,0:T(1,128)S(1)}, f32[8,4,1,512]{3,2,1,0:T(1,128)S(1)}, u32[]{:S(2)}, u32[]{:S(2)}) %collective-permute-start.5) | collective-permute-done | bytes 65568 | tf_op jit(solution)/shard_map/ppermute | solution.py:56
  24.2 3.3 %collective-permute-start.6 = (f32[8,1,8,512]{3,2,1,0:T(8,128)S(1)}, f32[8,1,8,512]{3,2,1,0:T(8,128)S(1)}, u32[]{:S(2)}, u32[]{:S(2)}) collective-permute-start(f32[8,1,8,512]{3,2,1,0:T(8,128)S(1)} %get-tuple-element.318), channel_id=1, source_target_pairs={{4,0},{8,4},{12,8},{16,12},{20,16},{24,20},{28,24},{5,1},{9,5},{13... | collective-permute-start | bytes 393224 | tf_op jit(solution)/shard_map/ppermute | solution.py:58
  27.4 3.5 %collective-permute-start.7 = (f32[8,1,8,512]{3,2,1,0:T(8,128)S(1)}, f32[8,1,8,512]{3,2,1,0:T(8,128)S(1)}, u32[]{:S(2)}, u32[]{:S(2)}) collective-permute-start(f32[8,1,8,512]{3,2,1,0:T(8,128)S(1)} %get-tuple-element.317), channel_id=1, source_target_pairs={{0,4},{4,8},{8,12},{12,16},{16,20},{20,24},{24,28},{1,5},{5,9},{9,... | collective-permute-start | bytes 393224 | tf_op jit(solution)/shard_map/ppermute | solution.py:56
  32.0 2.3 collective-permute-done.7
  36.3 2.4 collective-permute-start.9
  38.9 3.0 %collective-permute-done.9 = f32[8,4,1,512]{3,2,1,0:T(1,128)S(1)} collective-permute-done((f32[8,4,1,512]{3,2,1,0:T(1,128)S(1)}, f32[8,4,1,512]{3,2,1,0:T(1,128)S(1)}, u32[]{:S(2)}, u32[]{:S(2)}) %collective-permute-start.9) | collective-permute-done | bytes 65568 | tf_op jit(solution)/shard_map/ppermute | solution.py:56
  42.2 1.9 collective-permute-start.10
  44.1 4.8 %collective-permute-start.11 = (f32[8,1,8,512]{3,2,1,0:T(8,128)S(1)}, f32[8,1,8,512]{3,2,1,0:T(8,128)S(1)}, u32[]{:S(2)}, u32[]{:S(2)}) collective-permute-start(f32[8,1,8,512]{3,2,1,0:T(8,128)S(1)} %get-tuple-element.313), channel_id=1, source_target_pairs={{0,4},{4,8},{8,12},{12,16},{16,20},{20,24},{24,28},{1,5},{5,9},{9,... | collective-permute-start | bytes 393224 | tf_op jit(solution)/shard_map/ppermute | solution.py:56
  53.5 2.4 collective-permute-start.13
  56.1 3.0 %collective-permute-done.13 = f32[8,4,1,512]{3,2,1,0:T(1,128)S(1)} collective-permute-done((f32[8,4,1,512]{3,2,1,0:T(1,128)S(1)}, f32[8,4,1,512]{3,2,1,0:T(1,128)S(1)}, u32[]{:S(2)}, u32[]{:S(2)}) %collective-permute-start.13) | collective-permute-done | bytes 65568 | tf_op jit(solution)/shard_map/ppermute | solution.py:56
  59.5 2.5 while.30
  62.1 3.6 %collective-permute-done.14 = f32[1,8,128]{2,1,0:T(8,128)S(1)} collective-permute-done((f32[1,8,128]{2,1,0:T(8,128)S(1)}, f32[1,8,128]{2,1,0:T(8,128)S(1)}, u32[]{:S(2)}, u32[]{:S(2)}) %collective-permute-start.14) | collective-permute-done | bytes 4128 | tf_op jit(solution)/shard_map/ppermute | solution.py:34
  65.7 2.5 collective-permute-start.15
  69.9 3.0 %collective-permute-start.16 = (f32[4,8,128]{2,1,0:T(8,128)S(1)}, f32[4,8,128]{2,1,0:T(8,128)S(1)}, u32[]{:S(2)}, u32[]{:S(2)}) collective-permute-start(f32[4,8,128]{2,1,0:T(8,128)S(1)} %bitcast.99), channel_id=1, source_target_pairs={{0,16},{4,20},{8,24},{12,28},{16,0},{20,4},{24,8},{28,12},{1,17},{... | collective-permute-start | bytes 49160 | tf_op jit(solution)/shard_map/ppermute | solution.py:34
  75.3 27.7 %gather_fusion.1 = f32[8192,8]{1,0:T(8,128)} fusion(f32[8,128]{0,1:T(8,128)S(1)} %copy.12, s32[8192]{0:T(1024)S(1)} %fusion.122), kind=kCustom, calls=%fused_computation.clone | custom fusion | bytes 557056 | tf_op jit(solution)/shard_map/jit(_take)/gather | solution.py:189
  102.9 7.4 %broadcast_select_fusion.1 = f32[8192,8]{1,0:T(8,128)} fusion(f32[8192,8]{1,0:T(8,128)} %gather_fusion.1, pred[8192]{0:T(1024)(128)(4,1)S(1)} %compare_and_fusion), kind=kLoop, calls=%fused_computation.16 | loop fusion | flops 65536 | bytes 532480 | tf_op jit(solution)/shard_map/jit(_take)/select_n | solution.py:189
  110.4 2.8 %copy.13 = f32[8,2,8,512]{3,2,1,0:T(8,128)S(1)} copy(f32[8,2,8,512]{0,3,2,1:T(8,128)} %bitcast.93) | data formatting | bytes 524288 | tf_op jit(solution)/shard_map/reshape | solution.py:189
  113.3 3.3 %collective-permute-start.17 = (f32[8,1,8,512]{3,2,1,0:T(8,128)S(1)}, f32[8,1,8,512]{3,2,1,0:T(8,128)S(1)}, u32[]{:S(2)}, u32[]{:S(2)}) collective-permute-start(f32[8,1,8,512]{3,2,1,0:T(8,128)S(1)} %get-tuple-element.310), channel_id=1, source_target_pairs={{4,0},{8,4},{12,8},{16,12},{20,16},{24,20},{28,24},{5,1},{9,5},{13... | collective-permute-start | bytes 393224 | tf_op jit(solution)/shard_map/ppermute | solution.py:58
  116.6 3.5 %collective-permute-start.18 = (f32[8,1,8,512]{3,2,1,0:T(8,128)S(1)}, f32[8,1,8,512]{3,2,1,0:T(8,128)S(1)}, u32[]{:S(2)}, u32[]{:S(2)}) collective-permute-start(f32[8,1,8,512]{3,2,1,0:T(8,128)S(1)} %get-tuple-element.309), channel_id=1, source_target_pairs={{0,4},{4,8},{8,12},{12,16},{16,20},{20,24},{24,28},{1,5},{5,9},{9,... | collective-permute-start | bytes 393224 | tf_op jit(solution)/shard_map/ppermute | solution.py:56
  121.1 2.4 collective-permute-done.18
  125.5 2.4 collective-permute-start.20
  128.0 3.0 %collective-permute-done.20 = f32[8,4,1,512]{3,2,1,0:T(1,128)S(1)} collective-permute-done((f32[8,4,1,512]{3,2,1,0:T(1,128)S(1)}, f32[8,4,1,512]{3,2,1,0:T(1,128)S(1)}, u32[]{:S(2)}, u32[]{:S(2)}) %collective-permute-start.20) | collective-permute-done | bytes 65568 | tf_op jit(solution)/shard_map/ppermute | solution.py:56
  133.3 4.8 %collective-permute-start.22 = (f32[8,1,8,512]{3,2,1,0:T(8,128)S(1)}, f32[8,1,8,512]{3,2,1,0:T(8,128)S(1)}, u32[]{:S(2)}, u32[]{:S(2)}) collective-permute-start(f32[8,1,8,512]{3,2,1,0:T(8,128)S(1)} %get-tuple-element.305), channel_id=1, source_target_pairs={{0,4},{4,8},{8,12},{12,16},{16,20},{20,24},{24,28},{1,5},{5,9},{9,... | collective-permute-start | bytes 393224 | tf_op jit(solution)/shard_map/ppermute | solution.py:56
  142.6 2.4 collective-permute-start.24
  145.2 3.0 %collective-permute-done.24 = f32[8,4,1,512]{3,2,1,0:T(1,128)S(1)} collective-permute-done((f32[8,4,1,512]{3,2,1,0:T(1,128)S(1)}, f32[8,4,1,512]{3,2,1,0:T(1,128)S(1)}, u32[]{:S(2)}, u32[]{:S(2)}) %collective-permute-start.24) | collective-permute-done | bytes 65568 | tf_op jit(solution)/shard_map/ppermute | solution.py:56
  150.5 5.3 %collective-permute-start.26 = (f32[8,1,8,512]{3,2,1,0:T(8,128)S(1)}, f32[8,1,8,512]{3,2,1,0:T(8,128)S(1)}, u32[]{:S(2)}, u32[]{:S(2)}) collective-permute-start(f32[8,1,8,512]{3,2,1,0:T(8,128)S(1)} %get-tuple-element.301), channel_id=1, source_target_pairs={{0,4},{4,8},{8,12},{12,16},{16,20},{20,24},{24,28},{1,5},{5,9},{9,... | collective-permute-start | bytes 393224 | tf_op jit(solution)/shard_map/ppermute | solution.py:56
  160.3 2.4 collective-permute-start.28
  162.9 3.0 %collective-permute-done.28 = f32[8,4,1,512]{3,2,1,0:T(1,128)S(1)} collective-permute-done((f32[8,4,1,512]{3,2,1,0:T(1,128)S(1)}, f32[8,4,1,512]{3,2,1,0:T(1,128)S(1)}, u32[]{:S(2)}, u32[]{:S(2)}) %collective-permute-start.28) | collective-permute-done | bytes 65568 | tf_op jit(solution)/shard_map/ppermute | solution.py:56
  168.1 5.2 %collective-permute-start.30 = (f32[8,1,8,512]{3,2,1,0:T(8,128)S(1)}, f32[8,1,8,512]{3,2,1,0:T(8,128)S(1)}, u32[]{:S(2)}, u32[]{:S(2)}) collective-permute-start(f32[8,1,8,512]{3,2,1,0:T(8,128)S(1)} %get-tuple-element.297), channel_id=1, source_target_pairs={{0,4},{4,8},{8,12},{12,16},{16,20},{20,24},{24,28},{1,5},{5,9},{9,... | collective-permute-start | bytes 393224 | tf_op jit(solution)/shard_map/ppermute | solution.py:56
  177.9 2.6 %collective-permute-start.32 = (f32[8,4,1,512]{3,2,1,0:T(1,128)S(1)}, f32[8,4,1,512]{3,2,1,0:T(1,128)S(1)}, u32[]{:S(2)}, u32[]{:S(2)}) collective-permute-start(f32[8,4,1,512]{3,2,1,0:T(1,128)S(1)} %get-tuple-element.275), channel_id=1, source_target_pairs={{0,1},{1,2},{2,3},{4,5},{5,6},{6,7},{8,9},{9,10},{10,11},{12,13},{... | collective-permute-start | bytes 196616 | tf_op jit(solution)/shard_map/ppermute | solution.py:56
  180.7 2.8 %collective-permute-done.32 = f32[8,4,1,512]{3,2,1,0:T(1,128)S(1)} collective-permute-done((f32[8,4,1,512]{3,2,1,0:T(1,128)S(1)}, f32[8,4,1,512]{3,2,1,0:T(1,128)S(1)}, u32[]{:S(2)}, u32[]{:S(2)}) %collective-permute-start.32) | collective-permute-done | bytes 65568 | tf_op jit(solution)/shard_map/ppermute | solution.py:56
  183.9 2.5 while.31
  186.5 3.6 %collective-permute-done.33 = f32[1,8,128]{2,1,0:T(8,128)S(1)} collective-permute-done((f32[1,8,128]{2,1,0:T(8,128)S(1)}, f32[1,8,128]{2,1,0:T(8,128)S(1)}, u32[]{:S(2)}, u32[]{:S(2)}) %collective-permute-start.33) | collective-permute-done | bytes 4128 | tf_op jit(solution)/shard_map/ppermute | solution.py:34
  190.1 2.9 %collective-permute-start.34 = (f32[2,8,128]{2,1,0:T(8,128)S(1)}, f32[2,8,128]{2,1,0:T(8,128)S(1)}, u32[]{:S(2)}, u32[]{:S(2)}) collective-permute-start(f32[2,8,128]{2,1,0:T(8,128)S(1)} %get-tuple-element.326), channel_id=1, source_target_pairs={{0,8},{4,12},{8,0},{12,4},{16,24},{20,28},{24,16},{28,20},{1,9},{5... | collective-permute-start | bytes 24584 | tf_op jit(solution)/shard_map/ppermute | solution.py:34
  194.7 3.6 %collective-permute-start.35 = (f32[4,8,128]{2,1,0:T(8,128)S(1)}, f32[4,8,128]{2,1,0:T(8,128)S(1)}, u32[]{:S(2)}, u32[]{:S(2)}) collective-permute-start(f32[4,8,128]{2,1,0:T(8,128)S(1)} %bitcast.101), channel_id=1, source_target_pairs={{0,16},{4,20},{8,24},{12,28},{16,0},{20,4},{24,8},{28,12},{1,17},{... | collective-permute-start | bytes 49160 | tf_op jit(solution)/shard_map/ppermute | solution.py:34
  200.6 27.7 %gather_fusion.2 = f32[8192,8]{1,0:T(8,128)} fusion(f32[8,128]{0,1:T(8,128)S(1)} %copy.15, s32[8192]{0:T(1024)S(1)} %fusion.122), kind=kCustom, calls=%fused_computation.1.clone | custom fusion | bytes 557056 | tf_op jit(solution)/shard_map/jit(_take)/gather | solution.py:189
  228.3 7.4 %broadcast_select_fusion = f32[8192,8]{1,0:T(8,128)} fusion(f32[8192,8]{1,0:T(8,128)} %gather_fusion.2, pred[8192]{0:T(1024)(128)(4,1)S(1)} %compare_and_fusion), kind=kLoop, calls=%fused_computation.15 | loop fusion | flops 65536 | bytes 532480 | tf_op jit(solution)/shard_map/jit(_take)/select_n | solution.py:189
  235.7 2.8 %copy.16 = f32[8,2,8,512]{3,2,1,0:T(8,128)S(1)} copy(f32[8,2,8,512]{0,3,2,1:T(8,128)} %bitcast.92) | data formatting | bytes 524288 | tf_op jit(solution)/shard_map/reshape | solution.py:189
  238.6 3.3 %collective-permute-start.36 = (f32[8,1,8,512]{3,2,1,0:T(8,128)S(1)}, f32[8,1,8,512]{3,2,1,0:T(8,128)S(1)}, u32[]{:S(2)}, u32[]{:S(2)}) collective-permute-start(f32[8,1,8,512]{3,2,1,0:T(8,128)S(1)} %get-tuple-element.294), channel_id=1, source_target_pairs={{4,0},{8,4},{12,8},{16,12},{20,16},{24,20},{28,24},{5,1},{9,5},{13... | collective-permute-start | bytes 393224 | tf_op jit(solution)/shard_map/ppermute | solution.py:58
  241.9 3.5 %collective-permute-start.37 = (f32[8,1,8,512]{3,2,1,0:T(8,128)S(1)}, f32[8,1,8,512]{3,2,1,0:T(8,128)S(1)}, u32[]{:S(2)}, u32[]{:S(2)}) collective-permute-start(f32[8,1,8,512]{3,2,1,0:T(8,128)S(1)} %get-tuple-element.293), channel_id=1, source_target_pairs={{0,4},{4,8},{8,12},{12,16},{16,20},{20,24},{24,28},{1,5},{5,9},{9,... | collective-permute-start | bytes 393224 | tf_op jit(solution)/shard_map/ppermute | solution.py:56
  246.4 2.4 collective-permute-done.37
  250.8 2.4 collective-permute-start.39
  253.3 3.0 %collective-permute-done.39 = f32[8,4,1,512]{3,2,1,0:T(1,128)S(1)} collective-permute-done((f32[8,4,1,512]{3,2,1,0:T(1,128)S(1)}, f32[8,4,1,512]{3,2,1,0:T(1,128)S(1)}, u32[]{:S(2)}, u32[]{:S(2)}) %collective-permute-start.39) | collective-permute-done | bytes 65568 | tf_op jit(solution)/shard_map/ppermute | solution.py:56
  (139 shorter events, 57.0 us)
Async XLA Ops:
  0.0 49.0 %copy-start = (f32[1,128,1024]{2,1,0:T(8,128)S(1)}, f32[1,128,1024]{2,1,0:T(8,128)}, u32[]{:S(2)}) copy-start(f32[1,128,1024]{2,1,0:T(8,128)} %param.17) | copy-start | bytes 1572868
  0.0 16.2 %collective-permute-start.2 = (f32[8,1,8,512]{3,2,1,0:T(8,128)S(1)}, f32[8,1,8,512]{3,2,1,0:T(8,128)S(1)}, u32[]{:S(2)}, u32[]{:S(2)}) collective-permute-start(f32[8,1,8,512]{3,2,1,0:T(8,128)S(1)} %broadcast.145), channel_id=1, source_target_pairs={{4,0},{8,4},{12,8},{16,12},{20,16},{24,20},{28,24},{5,1},{9,5},{13... | collective-permute-start | bytes 393224 | tf_op jit(solution)/shard_map/ppermute | solution.py:58
  2.6 13.6 %collective-permute-start.3 = (f32[8,1,8,512]{3,2,1,0:T(8,128)S(1)}, f32[8,1,8,512]{3,2,1,0:T(8,128)S(1)}, u32[]{:S(2)}, u32[]{:S(2)}) collective-permute-start(f32[8,1,8,512]{3,2,1,0:T(8,128)S(1)} %broadcast.145), channel_id=1, source_target_pairs={{0,4},{4,8},{8,12},{12,16},{16,20},{20,24},{24,28},{1,5},{5,9},{9,... | collective-permute-start | bytes 393224 | tf_op jit(solution)/shard_map/ppermute | solution.py:56
  7.6 6.3 %collective-permute-start = (s32[1,8,512]{2,1,0:T(8,128)S(1)}, s32[1,8,512]{2,1,0:T(8,128)S(1)}, u32[]{:S(2)}, u32[]{:S(2)}) collective-permute-start(s32[1,8,512]{2,1,0:T(8,128)S(1)} %slice_bitcast_fusion.4), channel_id=1, source_target_pairs={{0,4},{4,8},{8,12},{12,16},{16,20},{20,24},{24,28},{1,5},{5,9},{9,... | collective-permute-start | bytes 49160 | tf_op jit(solution)/shard_map/ppermute | solution.py:68
  10.9 4.9 %collective-permute-start.1 = (s32[2,1,512]{2,1,0:T(1,128)S(1)}, s32[2,1,512]{2,1,0:T(1,128)S(1)}, u32[]{:S(2)}, u32[]{:S(2)}) collective-permute-start(s32[2,1,512]{2,1,0:T(1,128)S(1)} %slice_bitcast_fusion.5), channel_id=1, source_target_pairs={{0,1},{1,2},{2,3},{4,5},{5,6},{6,7},{8,9},{9,10},{10,11},{12,13},{... | collective-permute-start | bytes 12296 | tf_op jit(solution)/shard_map/ppermute | solution.py:68
  16.0 33.0 %copy-start.1 = (s32[2,8,512]{2,1,0:T(8,128)S(1)}, s32[2,8,512]{2,1,0:T(8,128)}, u32[]{:S(2)}) copy-start(s32[2,8,512]{2,1,0:T(8,128)} %param.16) | copy-start | bytes 98308
  16.3 4.4 %collective-permute-start.4 = (f32[8,4,1,512]{3,2,1,0:T(1,128)S(1)}, f32[8,4,1,512]{3,2,1,0:T(1,128)S(1)}, u32[]{:S(2)}, u32[]{:S(2)}) collective-permute-start(f32[8,4,1,512]{3,2,1,0:T(1,128)S(1)} %get-tuple-element.286), channel_id=1, source_target_pairs={{1,0},{2,1},{3,2},{5,4},{6,5},{7,6},{9,8},{10,9},{11,10},{13,12},{... | collective-permute-start | bytes 196616 | tf_op jit(solution)/shard_map/ppermute | solution.py:58
  18.3 5.6 %collective-permute-start.5 = (f32[8,4,1,512]{3,2,1,0:T(1,128)S(1)}, f32[8,4,1,512]{3,2,1,0:T(1,128)S(1)}, u32[]{:S(2)}, u32[]{:S(2)}) collective-permute-start(f32[8,4,1,512]{3,2,1,0:T(1,128)S(1)} %get-tuple-element.287), channel_id=1, source_target_pairs={{0,1},{1,2},{2,3},{4,5},{5,6},{6,7},{8,9},{9,10},{10,11},{12,13},{... | collective-permute-start | bytes 196616 | tf_op jit(solution)/shard_map/ppermute | solution.py:56
  24.2 7.9 %collective-permute-start.6 = (f32[8,1,8,512]{3,2,1,0:T(8,128)S(1)}, f32[8,1,8,512]{3,2,1,0:T(8,128)S(1)}, u32[]{:S(2)}, u32[]{:S(2)}) collective-permute-start(f32[8,1,8,512]{3,2,1,0:T(8,128)S(1)} %get-tuple-element.318), channel_id=1, source_target_pairs={{4,0},{8,4},{12,8},{16,12},{20,16},{24,20},{28,24},{5,1},{9,5},{13... | collective-permute-start | bytes 393224 | tf_op jit(solution)/shard_map/ppermute | solution.py:58
  27.4 6.9 %collective-permute-start.7 = (f32[8,1,8,512]{3,2,1,0:T(8,128)S(1)}, f32[8,1,8,512]{3,2,1,0:T(8,128)S(1)}, u32[]{:S(2)}, u32[]{:S(2)}) collective-permute-start(f32[8,1,8,512]{3,2,1,0:T(8,128)S(1)} %get-tuple-element.317), channel_id=1, source_target_pairs={{0,4},{4,8},{8,12},{12,16},{16,20},{20,24},{24,28},{1,5},{5,9},{9,... | collective-permute-start | bytes 393224 | tf_op jit(solution)/shard_map/ppermute | solution.py:56
  34.4 4.5 %collective-permute-start.8 = (f32[8,4,1,512]{3,2,1,0:T(1,128)S(1)}, f32[8,4,1,512]{3,2,1,0:T(1,128)S(1)}, u32[]{:S(2)}, u32[]{:S(2)}) collective-permute-start(f32[8,4,1,512]{3,2,1,0:T(1,128)S(1)} %get-tuple-element.284), channel_id=1, source_target_pairs={{1,0},{2,1},{3,2},{5,4},{6,5},{7,6},{9,8},{10,9},{11,10},{13,12},{... | collective-permute-start | bytes 196616 | tf_op jit(solution)/shard_map/ppermute | solution.py:58
  36.3 5.6 %collective-permute-start.9 = (f32[8,4,1,512]{3,2,1,0:T(1,128)S(1)}, f32[8,4,1,512]{3,2,1,0:T(1,128)S(1)}, u32[]{:S(2)}, u32[]{:S(2)}) collective-permute-start(f32[8,4,1,512]{3,2,1,0:T(1,128)S(1)} %get-tuple-element.285), channel_id=1, source_target_pairs={{0,1},{1,2},{2,3},{4,5},{5,6},{6,7},{8,9},{9,10},{10,11},{12,13},{... | collective-permute-start | bytes 196616 | tf_op jit(solution)/shard_map/ppermute | solution.py:56
  42.2 8.1 %collective-permute-start.10 = (f32[8,1,8,512]{3,2,1,0:T(8,128)S(1)}, f32[8,1,8,512]{3,2,1,0:T(8,128)S(1)}, u32[]{:S(2)}, u32[]{:S(2)}) collective-permute-start(f32[8,1,8,512]{3,2,1,0:T(8,128)S(1)} %get-tuple-element.314), channel_id=1, source_target_pairs={{4,0},{8,4},{12,8},{16,12},{20,16},{24,20},{28,24},{5,1},{9,5},{13... | collective-permute-start | bytes 393224 | tf_op jit(solution)/shard_map/ppermute | solution.py:58
  44.1 7.3 %collective-permute-start.11 = (f32[8,1,8,512]{3,2,1,0:T(8,128)S(1)}, f32[8,1,8,512]{3,2,1,0:T(8,128)S(1)}, u32[]{:S(2)}, u32[]{:S(2)}) collective-permute-start(f32[8,1,8,512]{3,2,1,0:T(8,128)S(1)} %get-tuple-element.313), channel_id=1, source_target_pairs={{0,4},{4,8},{8,12},{12,16},{16,20},{20,24},{24,28},{1,5},{5,9},{9,... | collective-permute-start | bytes 393224 | tf_op jit(solution)/shard_map/ppermute | solution.py:56
  51.6 4.5 %collective-permute-start.12 = (f32[8,4,1,512]{3,2,1,0:T(1,128)S(1)}, f32[8,4,1,512]{3,2,1,0:T(1,128)S(1)}, u32[]{:S(2)}, u32[]{:S(2)}) collective-permute-start(f32[8,4,1,512]{3,2,1,0:T(1,128)S(1)} %get-tuple-element.282), channel_id=1, source_target_pairs={{1,0},{2,1},{3,2},{5,4},{6,5},{7,6},{9,8},{10,9},{11,10},{13,12},{... | collective-permute-start | bytes 196616 | tf_op jit(solution)/shard_map/ppermute | solution.py:58
  53.5 5.6 %collective-permute-start.13 = (f32[8,4,1,512]{3,2,1,0:T(1,128)S(1)}, f32[8,4,1,512]{3,2,1,0:T(1,128)S(1)}, u32[]{:S(2)}, u32[]{:S(2)}) collective-permute-start(f32[8,4,1,512]{3,2,1,0:T(1,128)S(1)} %get-tuple-element.283), channel_id=1, source_target_pairs={{0,1},{1,2},{2,3},{4,5},{5,6},{6,7},{8,9},{9,10},{10,11},{12,13},{... | collective-permute-start | bytes 196616 | tf_op jit(solution)/shard_map/ppermute | solution.py:56
  62.0 3.7 %collective-permute-start.14 = (f32[1,8,128]{2,1,0:T(8,128)S(1)}, f32[1,8,128]{2,1,0:T(8,128)S(1)}, u32[]{:S(2)}, u32[]{:S(2)}) collective-permute-start(f32[1,8,128]{2,1,0:T(8,128)S(1)} %get-tuple-element.332), channel_id=1, source_target_pairs={{0,4},{4,0},{8,12},{12,8},{16,20},{20,16},{24,28},{28,24},{1,5},{5... | collective-permute-start | bytes 12296 | tf_op jit(solution)/shard_map/ppermute | solution.py:34
  65.7 4.2 %collective-permute-start.15 = (f32[2,8,128]{2,1,0:T(8,128)S(1)}, f32[2,8,128]{2,1,0:T(8,128)S(1)}, u32[]{:S(2)}, u32[]{:S(2)}) collective-permute-start(f32[2,8,128]{2,1,0:T(8,128)S(1)} %get-tuple-element.328), channel_id=1, source_target_pairs={{0,8},{4,12},{8,0},{12,4},{16,24},{20,28},{24,16},{28,20},{1,9},{5... | collective-permute-start | bytes 24584 | tf_op jit(solution)/shard_map/ppermute | solution.py:34
  69.9 4.8 %collective-permute-start.16 = (f32[4,8,128]{2,1,0:T(8,128)S(1)}, f32[4,8,128]{2,1,0:T(8,128)S(1)}, u32[]{:S(2)}, u32[]{:S(2)}) collective-permute-start(f32[4,8,128]{2,1,0:T(8,128)S(1)} %bitcast.99), channel_id=1, source_target_pairs={{0,16},{4,20},{8,24},{12,28},{16,0},{20,4},{24,8},{28,12},{1,17},{... | collective-permute-start | bytes 49160 | tf_op jit(solution)/shard_map/ppermute | solution.py:34
  113.3 7.8 %collective-permute-start.17 = (f32[8,1,8,512]{3,2,1,0:T(8,128)S(1)}, f32[8,1,8,512]{3,2,1,0:T(8,128)S(1)}, u32[]{:S(2)}, u32[]{:S(2)}) collective-permute-start(f32[8,1,8,512]{3,2,1,0:T(8,128)S(1)} %get-tuple-element.310), channel_id=1, source_target_pairs={{4,0},{8,4},{12,8},{16,12},{20,16},{24,20},{28,24},{5,1},{9,5},{13... | collective-permute-start | bytes 393224 | tf_op jit(solution)/shard_map/ppermute | solution.py:58
  116.6 6.9 %collective-permute-start.18 = (f32[8,1,8,512]{3,2,1,0:T(8,128)S(1)}, f32[8,1,8,512]{3,2,1,0:T(8,128)S(1)}, u32[]{:S(2)}, u32[]{:S(2)}) collective-permute-start(f32[8,1,8,512]{3,2,1,0:T(8,128)S(1)} %get-tuple-element.309), channel_id=1, source_target_pairs={{0,4},{4,8},{8,12},{12,16},{16,20},{20,24},{24,28},{1,5},{5,9},{9,... | collective-permute-start | bytes 393224 | tf_op jit(solution)/shard_map/ppermute | solution.py:56
  123.5 4.5 %collective-permute-start.19 = (f32[8,4,1,512]{3,2,1,0:T(1,128)S(1)}, f32[8,4,1,512]{3,2,1,0:T(1,128)S(1)}, u32[]{:S(2)}, u32[]{:S(2)}) collective-permute-start(f32[8,4,1,512]{3,2,1,0:T(1,128)S(1)} %get-tuple-element.280), channel_id=1, source_target_pairs={{1,0},{2,1},{3,2},{5,4},{6,5},{7,6},{9,8},{10,9},{11,10},{13,12},{... | collective-permute-start | bytes 196616 | tf_op jit(solution)/shard_map/ppermute | solution.py:58
  125.5 5.6 %collective-permute-start.20 = (f32[8,4,1,512]{3,2,1,0:T(1,128)S(1)}, f32[8,4,1,512]{3,2,1,0:T(1,128)S(1)}, u32[]{:S(2)}, u32[]{:S(2)}) collective-permute-start(f32[8,4,1,512]{3,2,1,0:T(1,128)S(1)} %get-tuple-element.281), channel_id=1, source_target_pairs={{0,1},{1,2},{2,3},{4,5},{5,6},{6,7},{8,9},{9,10},{10,11},{12,13},{... | collective-permute-start | bytes 196616 | tf_op jit(solution)/shard_map/ppermute | solution.py:56
  131.4 7.8 %collective-permute-start.21 = (f32[8,1,8,512]{3,2,1,0:T(8,128)S(1)}, f32[8,1,8,512]{3,2,1,0:T(8,128)S(1)}, u32[]{:S(2)}, u32[]{:S(2)}) collective-permute-start(f32[8,1,8,512]{3,2,1,0:T(8,128)S(1)} %get-tuple-element.306), channel_id=1, source_target_pairs={{4,0},{8,4},{12,8},{16,12},{20,16},{24,20},{28,24},{5,1},{9,5},{13... | collective-permute-start | bytes 393224 | tf_op jit(solution)/shard_map/ppermute | solution.py:58
  133.3 7.3 %collective-permute-start.22 = (f32[8,1,8,512]{3,2,1,0:T(8,128)S(1)}, f32[8,1,8,512]{3,2,1,0:T(8,128)S(1)}, u32[]{:S(2)}, u32[]{:S(2)}) collective-permute-start(f32[8,1,8,512]{3,2,1,0:T(8,128)S(1)} %get-tuple-element.305), channel_id=1, source_target_pairs={{0,4},{4,8},{8,12},{12,16},{16,20},{20,24},{24,28},{1,5},{5,9},{9,... | collective-permute-start | bytes 393224 | tf_op jit(solution)/shard_map/ppermute | solution.py:56
  140.7 4.5 %collective-permute-start.23 = (f32[8,4,1,512]{3,2,1,0:T(1,128)S(1)}, f32[8,4,1,512]{3,2,1,0:T(1,128)S(1)}, u32[]{:S(2)}, u32[]{:S(2)}) collective-permute-start(f32[8,4,1,512]{3,2,1,0:T(1,128)S(1)} %get-tuple-element.278), channel_id=1, source_target_pairs={{1,0},{2,1},{3,2},{5,4},{6,5},{7,6},{9,8},{10,9},{11,10},{13,12},{... | collective-permute-start | bytes 196616 | tf_op jit(solution)/shard_map/ppermute | solution.py:58
  142.6 5.6 %collective-permute-start.24 = (f32[8,4,1,512]{3,2,1,0:T(1,128)S(1)}, f32[8,4,1,512]{3,2,1,0:T(1,128)S(1)}, u32[]{:S(2)}, u32[]{:S(2)}) collective-permute-start(f32[8,4,1,512]{3,2,1,0:T(1,128)S(1)} %get-tuple-element.279), channel_id=1, source_target_pairs={{0,1},{1,2},{2,3},{4,5},{5,6},{6,7},{8,9},{9,10},{10,11},{12,13},{... | collective-permute-start | bytes 196616 | tf_op jit(solution)/shard_map/ppermute | solution.py:56
  148.5 8.3 %collective-permute-start.25 = (f32[8,1,8,512]{3,2,1,0:T(8,128)S(1)}, f32[8,1,8,512]{3,2,1,0:T(8,128)S(1)}, u32[]{:S(2)}, u32[]{:S(2)}) collective-permute-start(f32[8,1,8,512]{3,2,1,0:T(8,128)S(1)} %get-tuple-element.302), channel_id=1, source_target_pairs={{4,0},{8,4},{12,8},{16,12},{20,16},{24,20},{28,24},{5,1},{9,5},{13... | collective-permute-start | bytes 393224 | tf_op jit(solution)/shard_map/ppermute | solution.py:58
  150.5 7.8 %collective-permute-start.26 = (f32[8,1,8,512]{3,2,1,0:T(8,128)S(1)}, f32[8,1,8,512]{3,2,1,0:T(8,128)S(1)}, u32[]{:S(2)}, u32[]{:S(2)}) collective-permute-start(f32[8,1,8,512]{3,2,1,0:T(8,128)S(1)} %get-tuple-element.301), channel_id=1, source_target_pairs={{0,4},{4,8},{8,12},{12,16},{16,20},{20,24},{24,28},{1,5},{5,9},{9,... | collective-permute-start | bytes 393224 | tf_op jit(solution)/shard_map/ppermute | solution.py:56
  158.4 4.5 %collective-permute-start.27 = (f32[8,4,1,512]{3,2,1,0:T(1,128)S(1)}, f32[8,4,1,512]{3,2,1,0:T(1,128)S(1)}, u32[]{:S(2)}, u32[]{:S(2)}) collective-permute-start(f32[8,4,1,512]{3,2,1,0:T(1,128)S(1)} %get-tuple-element.276), channel_id=1, source_target_pairs={{1,0},{2,1},{3,2},{5,4},{6,5},{7,6},{9,8},{10,9},{11,10},{13,12},{... | collective-permute-start | bytes 196616 | tf_op jit(solution)/shard_map/ppermute | solution.py:58
  160.3 5.6 %collective-permute-start.28 = (f32[8,4,1,512]{3,2,1,0:T(1,128)S(1)}, f32[8,4,1,512]{3,2,1,0:T(1,128)S(1)}, u32[]{:S(2)}, u32[]{:S(2)}) collective-permute-start(f32[8,4,1,512]{3,2,1,0:T(1,128)S(1)} %get-tuple-element.277), channel_id=1, source_target_pairs={{0,1},{1,2},{2,3},{4,5},{5,6},{6,7},{8,9},{9,10},{10,11},{12,13},{... | collective-permute-start | bytes 196616 | tf_op jit(solution)/shard_map/ppermute | solution.py:56
  166.2 8.2 %collective-permute-start.29 = (f32[8,1,8,512]{3,2,1,0:T(8,128)S(1)}, f32[8,1,8,512]{3,2,1,0:T(8,128)S(1)}, u32[]{:S(2)}, u32[]{:S(2)}) collective-permute-start(f32[8,1,8,512]{3,2,1,0:T(8,128)S(1)} %get-tuple-element.298), channel_id=1, source_target_pairs={{4,0},{8,4},{12,8},{16,12},{20,16},{24,20},{28,24},{5,1},{9,5},{13... | collective-permute-start | bytes 393224 | tf_op jit(solution)/shard_map/ppermute | solution.py:58
  168.1 7.8 %collective-permute-start.30 = (f32[8,1,8,512]{3,2,1,0:T(8,128)S(1)}, f32[8,1,8,512]{3,2,1,0:T(8,128)S(1)}, u32[]{:S(2)}, u32[]{:S(2)}) collective-permute-start(f32[8,1,8,512]{3,2,1,0:T(8,128)S(1)} %get-tuple-element.297), channel_id=1, source_target_pairs={{0,4},{4,8},{8,12},{12,16},{16,20},{20,24},{24,28},{1,5},{5,9},{9,... | collective-permute-start | bytes 393224 | tf_op jit(solution)/shard_map/ppermute | solution.py:56
  176.0 4.7 %collective-permute-start.31 = (f32[8,4,1,512]{3,2,1,0:T(1,128)S(1)}, f32[8,4,1,512]{3,2,1,0:T(1,128)S(1)}, u32[]{:S(2)}, u32[]{:S(2)}) collective-permute-start(f32[8,4,1,512]{3,2,1,0:T(1,128)S(1)} %get-tuple-element.274), channel_id=1, source_target_pairs={{1,0},{2,1},{3,2},{5,4},{6,5},{7,6},{9,8},{10,9},{11,10},{13,12},{... | collective-permute-start | bytes 196616 | tf_op jit(solution)/shard_map/ppermute | solution.py:58
  177.9 5.6 %collective-permute-start.32 = (f32[8,4,1,512]{3,2,1,0:T(1,128)S(1)}, f32[8,4,1,512]{3,2,1,0:T(1,128)S(1)}, u32[]{:S(2)}, u32[]{:S(2)}) collective-permute-start(f32[8,4,1,512]{3,2,1,0:T(1,128)S(1)} %get-tuple-element.275), channel_id=1, source_target_pairs={{0,1},{1,2},{2,3},{4,5},{5,6},{6,7},{8,9},{9,10},{10,11},{12,13},{... | collective-permute-start | bytes 196616 | tf_op jit(solution)/shard_map/ppermute | solution.py:56
  186.4 3.7 %collective-permute-start.33 = (f32[1,8,128]{2,1,0:T(8,128)S(1)}, f32[1,8,128]{2,1,0:T(8,128)S(1)}, u32[]{:S(2)}, u32[]{:S(2)}) collective-permute-start(f32[1,8,128]{2,1,0:T(8,128)S(1)} %get-tuple-element.330), channel_id=1, source_target_pairs={{0,4},{4,0},{8,12},{12,8},{16,20},{20,16},{24,28},{28,24},{1,5},{5... | collective-permute-start | bytes 12296 | tf_op jit(solution)/shard_map/ppermute | solution.py:34
  190.1 4.5 %collective-permute-start.34 = (f32[2,8,128]{2,1,0:T(8,128)S(1)}, f32[2,8,128]{2,1,0:T(8,128)S(1)}, u32[]{:S(2)}, u32[]{:S(2)}) collective-permute-start(f32[2,8,128]{2,1,0:T(8,128)S(1)} %get-tuple-element.326), channel_id=1, source_target_pairs={{0,8},{4,12},{8,0},{12,4},{16,24},{20,28},{24,16},{28,20},{1,9},{5... | collective-permute-start | bytes 24584 | tf_op jit(solution)/shard_map/ppermute | solution.py:34
  194.7 5.3 %collective-permute-start.35 = (f32[4,8,128]{2,1,0:T(8,128)S(1)}, f32[4,8,128]{2,1,0:T(8,128)S(1)}, u32[]{:S(2)}, u32[]{:S(2)}) collective-permute-start(f32[4,8,128]{2,1,0:T(8,128)S(1)} %bitcast.101), channel_id=1, source_target_pairs={{0,16},{4,20},{8,24},{12,28},{16,0},{20,4},{24,8},{28,12},{1,17},{... | collective-permute-start | bytes 49160 | tf_op jit(solution)/shard_map/ppermute | solution.py:34
  238.6 7.8 %collective-permute-start.36 = (f32[8,1,8,512]{3,2,1,0:T(8,128)S(1)}, f32[8,1,8,512]{3,2,1,0:T(8,128)S(1)}, u32[]{:S(2)}, u32[]{:S(2)}) collective-permute-start(f32[8,1,8,512]{3,2,1,0:T(8,128)S(1)} %get-tuple-element.294), channel_id=1, source_target_pairs={{4,0},{8,4},{12,8},{16,12},{20,16},{24,20},{28,24},{5,1},{9,5},{13... | collective-permute-start | bytes 393224 | tf_op jit(solution)/shard_map/ppermute | solution.py:58
  241.9 6.9 %collective-permute-start.37 = (f32[8,1,8,512]{3,2,1,0:T(8,128)S(1)}, f32[8,1,8,512]{3,2,1,0:T(8,128)S(1)}, u32[]{:S(2)}, u32[]{:S(2)}) collective-permute-start(f32[8,1,8,512]{3,2,1,0:T(8,128)S(1)} %get-tuple-element.293), channel_id=1, source_target_pairs={{0,4},{4,8},{8,12},{12,16},{16,20},{20,24},{24,28},{1,5},{5,9},{9,... | collective-permute-start | bytes 393224 | tf_op jit(solution)/shard_map/ppermute | solution.py:56
  248.9 4.5 %collective-permute-start.38 = (f32[8,4,1,512]{3,2,1,0:T(1,128)S(1)}, f32[8,4,1,512]{3,2,1,0:T(1,128)S(1)}, u32[]{:S(2)}, u32[]{:S(2)}) collective-permute-start(f32[8,4,1,512]{3,2,1,0:T(1,128)S(1)} %get-tuple-element.272), channel_id=1, source_target_pairs={{1,0},{2,1},{3,2},{5,4},{6,5},{7,6},{9,8},{10,9},{11,10},{13,12},{... | collective-permute-start | bytes 196616 | tf_op jit(solution)/shard_map/ppermute | solution.py:58
  250.8 5.6 %collective-permute-start.39 = (f32[8,4,1,512]{3,2,1,0:T(1,128)S(1)}, f32[8,4,1,512]{3,2,1,0:T(1,128)S(1)}, u32[]{:S(2)}, u32[]{:S(2)}) collective-permute-start(f32[8,4,1,512]{3,2,1,0:T(1,128)S(1)} %get-tuple-element.273), channel_id=1, source_target_pairs={{0,1},{1,2},{2,3},{4,5},{5,6},{6,7},{8,9},{9,10},{10,11},{12,13},{... | collective-permute-start | bytes 196616 | tf_op jit(solution)/shard_map/ppermute | solution.py:56
